TPU v7x, 256 devices: a whole 4x4x8 slice. The times are simulated.
256 devices in a mesh: rep: 32 (over y, z), hx: 8 (over x, core).
Axes of the slice: x: 4, y: 4, z: 8, core: 2. Of those that a mesh axis runs over, the one named last changes fastest.
Arguments:
- stream_in: bfloat16 [768, 6144], P(None, 'rep'), may hold values from -6 to 6
- query: bfloat16 [768, 6144], P('rep', 'hx'), may hold values from -240 to 240
- new_kv: bfloat16 [768, 2, 1024], P('rep', None, 'hx'), may hold values from -6 to 6
- cache: bfloat16 [768, 2, 128, 1024], P('rep', None, None, 'hx'), may hold values from -127 to 127, as said below
- precision: int32 [768, 4], P('rep'), may hold values from 0 to 1
- cache_scale: float32 [768, 2, 4, 8], P('rep', None, None, 'hx'), may hold values from 0.004 to 0.03
- lengths: int32 [768], P('rep'), may hold values from 0 to 128
- w_heads: bfloat16 [6144, 6144], P('hx', 'rep'), may hold values from -0.3125 to 0.3125
- norm_gain: float32 [6144], P('rep'), may hold values from 0.5 to 1.5
- w_router: bfloat16 [6144, 8], P('rep'), may hold values from -0.0390625 to 0.0390625
- expert_choice: int32 [768, 2], replicated, may hold values from 0 to 7, all different within a row; in each aligned block of 768 rows (0 to 767, 768 to 1535, ...) at most 384 rows name the same one
- w_in: bfloat16 [8, 6144, 2, 8192], P('hx', None, None, 'rep'), may hold values from -0.078125 to 0.078125
- w_down: bfloat16 [8, 8192, 6144], P('hx', 'rep'), may hold values from -0.0625 to 0.0625
- mig_dest: int32 [32], replicated, may hold values from 0 to 31, as said below
- mig_req: int32 [32], replicated, may hold values from 0 to 23
- mig_blocks: int32 [32], replicated, may hold values from 1 to 4
Outputs:
- mixed: bfloat16 [768, 6144], P(None, 'rep')
- arrived: bfloat16 [32, 2, 2, 128, 1024], P('rep', None, None, None, 'hx')
Inputs may be any that keep to these rules, and one draw needn't show every extreme that they name: `cache`: in blocks whose precision entry is 1, the stored values are whole numbers. `expert_choice`: each row names two different experts; over all 768 rows no expert is named by more than 384 rows, a bound that some block reaches. `mig_dest`: no replica names itself; no replica is named by more than 2 replicas, and one is named by exactly 2.
All inputs are finite; a program needn't handle non-finite values.
Results may differ from a plain program's by a relative error of at most 0.0065.
Values may be sent and summed in bfloat16 or wider, within the bound.
A program may use at most 128 MiB of HBM per device.

v0:
```python
import jax
import jax.numpy as jnp
from jax import lax
from jax.sharding import PartitionSpec as P

D = 6144
HEAD = 128
GROUP = 6
BLOCK_LEN = 32
IN_MOST = 2
CACHE = 128
EPSILON = 1e-05


def from_everyone(x, axis):
    copies = jnp.broadcast_to(x, (lax.axis_size(axis), *x.shape))
    return lax.all_to_all(copies, axis, split_axis=0, concat_axis=0, tiled=True)


def in_order(blocks, dim):
    blocks = jnp.moveaxis(blocks, 0, dim)
    lengths = blocks.shape
    return blocks.reshape(*lengths[:dim], lengths[dim] * lengths[dim + 1], *lengths[dim + 2 :])


def gather_directly(x, axis, dim):
    blocks = from_everyone(x, axis)
    return in_order(blocks, dim)


def taken_together(x, axis):
    return from_everyone(x, axis).sum(axis=0)


def over_copies(x, axis):
    everything = from_everyone(x, axis)
    return jnp.sum(everything.astype(jnp.float32), axis=0)


def block_factor(precision, cache_scale):
    factor = jnp.where(precision[:, None, :, None] == 1, cache_scale, 1.0)
    return jnp.repeat(factor, BLOCK_LEN, axis=2)


def attend(query, new_kv, cache, factor, lengths):
    rows = query.shape[0]
    heads_kv = new_kv.shape[2] // HEAD
    scale = HEAD ** (-0.5)
    queries = query.reshape(rows, heads_kv, GROUP, HEAD)
    keys = cache[:, 0].reshape(rows, CACHE, heads_kv, HEAD)
    values = cache[:, 1].reshape(rows, CACHE, heads_kv, HEAD)
    fresh = new_kv.reshape(rows, 2, heads_kv, HEAD)
    scores = jnp.einsum("rkgd,rpkd->rkgp", queries, keys, preferred_element_type=jnp.float32)
    scores = scores * jnp.transpose(factor[:, 0], (0, 2, 1))[:, :, None, :] * scale
    own = (
        jnp.einsum("rkgd,rkd->rkg", queries, fresh[:, 0], preferred_element_type=jnp.float32)
        * scale
    )
    live = jnp.arange(CACHE)[None, :] < lengths[:, None]
    scores = jnp.where(live[:, None, None, :], scores, -jnp.inf)
    top = jnp.maximum(jnp.max(scores, axis=3), own)
    weights = jnp.exp(scores - top[..., None])
    own_weight = jnp.exp(own - top)
    total = jnp.sum(weights, axis=3) + own_weight
    value_weight = (
        weights / total[..., None] * jnp.transpose(factor[:, 1], (0, 2, 1))[:, :, None, :]
    ).astype(jnp.bfloat16)
    own_prob = (own_weight / total).astype(jnp.bfloat16)
    result = jnp.einsum("rkgp,rpkd->rkgd", value_weight, values, preferred_element_type=jnp.float32)
    result = result + own_prob.astype(jnp.float32)[..., None] * fresh[:, 1][:, :, None, :].astype(
        jnp.float32
    )
    return result.reshape(rows, heads_kv * GROUP * HEAD).astype(jnp.bfloat16)


def local(
    stream_in,
    query,
    new_kv,
    cache,
    precision,
    cache_scale,
    lengths,
    w_heads,
    norm_gain,
    w_router,
    expert_choice,
    w_in,
    w_down,
    mig_dest,
    mig_req,
    mig_blocks,
):
    tokens = stream_in.shape[0]
    capacity = tokens // 2
    experts_all = w_router.shape[1]
    factor = block_factor(precision, cache_scale)
    attended = attend(query, new_kv, cache, factor, lengths)
    partial_value = jnp.dot(
        gather_directly(attended, "rep", 0), w_heads, preferred_element_type=jnp.float32
    )
    hidden_state = stream_in.astype(jnp.float32) + taken_together(partial_value, "hx")
    scaled = hidden_state * norm_gain[None, :]
    router_f32 = w_router.astype(jnp.float32)
    squares = taken_together(jnp.sum(hidden_state * hidden_state, axis=1), "rep")
    inverse = lax.rsqrt(squares / D + EPSILON)
    normed = scaled * inverse[:, None]
    logits = taken_together(jnp.dot(normed, router_f32, precision=lax.Precision.HIGHEST), "rep")
    onehot_choice = expert_choice[:, :, None] == jnp.arange(experts_all)[None, None, :]
    chosen = jnp.sum(jnp.where(onehot_choice, logits[:, None, :], 0.0), axis=2)
    peak = jnp.max(chosen, axis=1, keepdims=True)
    expo = jnp.exp(chosen - peak)
    gates = expo / jnp.sum(expo, axis=1, keepdims=True)
    u_rows = normed.astype(jnp.bfloat16)
    expert = lax.axis_index("hx")
    flat = expert_choice.reshape(-1)
    pair_token = jnp.arange(2 * tokens) // 2
    gate_flat = gates.reshape(-1)
    onehot = (flat[:, None] == jnp.arange(experts_all)[None, :]).astype(jnp.int32)
    rank = jnp.sum((jnp.cumsum(onehot, axis=0) - onehot) * onehot, axis=1)
    select = (flat[None, :] == expert) & (rank[None, :] == jnp.arange(capacity)[:, None])
    token_of_slot = jnp.sum(jnp.where(select, pair_token[None, :], 0), axis=1)
    live = jnp.any(select, axis=1)
    gate_of_slot = jnp.sum(jnp.where(select, gate_flat[None, :], 0.0), axis=1)
    match = (token_of_slot[:, None] == jnp.arange(tokens)[None, :]) & live[:, None]
    combine = jnp.where(match, gate_of_slot[:, None], 0.0)
    ff_local = w_in.shape[3]
    w_flat = w_in[0].reshape(D, 2 * ff_local)
    picked = jnp.where(live[:, None], u_rows[token_of_slot], jnp.zeros((), jnp.bfloat16))
    gate_up = jnp.dot(
        lax.all_gather(picked, "rep", axis=1, tiled=True),
        w_flat,
        preferred_element_type=jnp.float32,
    )
    act = (jax.nn.silu(gate_up[:, :ff_local]) * gate_up[:, ff_local:]).astype(jnp.bfloat16)
    down_rows = lax.all_to_all(w_down, "rep", split_axis=2, concat_axis=1, tiled=True)[0]
    expert_out = lax.dot_general(
        down_rows,
        lax.all_gather(act, "rep", axis=1, tiled=True),
        (((0,), (1,)), ((), ())),
        preferred_element_type=jnp.float32,
    )
    weighted = jnp.dot(expert_out, combine, precision=lax.Precision.HIGHEST)
    moe = over_copies(weighted.astype(jnp.bfloat16), "hx").astype(jnp.float32)
    mixed = (hidden_state + moe.T).astype(jnp.bfloat16)
    replica_id = lax.axis_index("rep")
    chosen_req = mig_req[replica_id]
    count = mig_blocks[replica_id]
    levels = lax.dynamic_index_in_dim(cache, chosen_req, 0, keepdims=False).astype(jnp.float32)
    scales = lax.dynamic_index_in_dim(factor, chosen_req, 0, keepdims=False)
    keep = jnp.arange(CACHE) < count * BLOCK_LEN
    outgoing = (
        jnp.where(keep[None, :, None], levels * scales, 0.0).astype(jnp.bfloat16).reshape(1, -1)
    )
    aimed = (mig_dest == replica_id).astype(jnp.int32)
    before = jnp.cumsum(aimed) - aimed
    slots = ((aimed[None, :] == 1) & (before[None, :] == jnp.arange(IN_MOST)[:, None])).astype(
        jnp.bfloat16
    )
    replicas = lax.axis_size("rep")
    target = mig_dest[replica_id]
    outbox = jnp.where(
        (jnp.arange(replicas) == target)[:, None], outgoing, jnp.zeros((), jnp.bfloat16)
    )
    received = lax.all_to_all(outbox, "rep", split_axis=0, concat_axis=0, tiled=True)
    arrived = jnp.dot(slots, received, preferred_element_type=jnp.float32)
    arrived = arrived.astype(jnp.bfloat16).reshape(1, IN_MOST, 2, CACHE, -1)
    return (mixed, arrived)


def solution(mesh):
    placed = (
        P(None, "rep"),
        P("rep", "hx"),
        P("rep", None, "hx"),
        P("rep", None, None, "hx"),
        P("rep", None),
        P("rep", None, None, "hx"),
        P("rep"),
        P("hx", "rep"),
        P("rep"),
        P("rep", None),
        P(),
        P("hx", None, None, "rep"),
        P("hx", "rep", None),
        P(),
        P(),
        P(),
    )
    return jax.shard_map(
        local,
        mesh=mesh,
        in_specs=placed,
        out_specs=(P(None, "rep"), P("rep", None, None, None, "hx")),
        check_vma=False,
    )
```

profile of v0, /device:TPU:1, one launch (start us, length us, event | category | flops | bytes accessed | tf_op | source)
XLA Modules:
  0.0 459.4 jit_solution(9098578894899218675)
XLA Ops:
  15.0 43.0 %all_to_all.50 = bf16[32,24,768]{2,1,0:T(8,128)(2,1)S(1)} all-to-all(bf16[32,24,768]{2,1,0:T(8,128)(2,1)S(1)} %broadcast_in_dim.173), channel_id=1, replica_groups=mesh['rep'=32,'hx'=8] {'rep'}, dimensions={0} | all-to-all | bytes 2359296 | tf_op jit(solution)/shard_map/all_to_all | solution.py:17
  61.1 7.3 %all-to-all-start.1 = ((f32[8,768,192]{1,2,0:T(8,128)}), f32[8,768,192]{1,2,0:T(8,128)}, u32[]{:S(2)}, u32[]{:S(2)}) async-start(f32[8,768,192]{1,2,0:T(8,128)} %broadcast_in_dim.174), calls=%async_computation.1 | async-start | bytes 9437184 | tf_op jit(solution)/shard_map/all_to_all | solution.py:17
  72.7 50.1 %all-to-all-done.1 = f32[8,768,192]{1,2,0:T(8,128)} async-done(((f32[8,768,192]{1,2,0:T(8,128)}), f32[8,768,192]{1,2,0:T(8,128)}, u32[]{:S(2)}, u32[]{:S(2)}) %all-to-all-start.1) | async-done | bytes 4718624 | tf_op jit(solution)/shard_map/all_to_all | solution.py:17
  131.0 8.6 %all-to-all-done.2 = f32[32,1,768]{2,1,0:T(1,128)S(1)} async-done(((f32[32,1,768]{2,1,0:T(1,128)}), f32[32,1,768]{2,1,0:T(1,128)S(1)}, u32[]{:S(2)}, u32[]{:S(2)}) %all-to-all-start.2) | async-done | bytes 98336 | tf_op jit(solution)/shard_map/all_to_all | solution.py:17
  142.9 14.0 %copy.94 = bf16[1,256,6144]{1,0,2:T(2,128)(2,1)} copy(bf16[1,256,6144]{2,1,0:T(8,128)(2,1)} %param.28) | data formatting | bytes 6291456 | tf_op args[12]
  157.3 33.3 %reduce.10 = bf16[6144,256]{1,0:T(8,128)(2,1)} reduce(bf16[6144,1,256]{2,1,0:T(2,128)(2,1)} %bitcast.106, bf16[]{:T(256)} %broadcast.197), dimensions={1}, to_apply=%bitcast.88.reduce_sub_computation | reduce | bytes 6291458
  190.6 7.8 %reshape.333 = bf16[32,2,24576]{2,1,0:T(2,128)(2,1)} reshape(bf16[6144,256]{1,0:T(8,128)(2,1)} %reduce.10) | data formatting | bytes 6291456
  198.5 4.8 %all-to-all-start.3 = ((bf16[32,2,24576]{2,1,0:T(2,128)(2,1)}), bf16[32,2,24576]{2,1,0:T(2,128)(2,1)}, u32[]{:S(2)}, u32[]{:S(2)}) async-start(bf16[32,2,24576]{2,1,0:T(2,128)(2,1)} %reshape.333), calls=%async_computation.3 | async-start | bytes 6291456 | tf_op jit(solution)/shard_map/all_to_all | solution.py:136
  203.5 6.6 %copy.109 = bf16[768,8,2,256]{3,1,2,0:T(8,128)(2,1)} copy(bf16[768,8,2,256]{3,2,1,0:T(2,128)(2,1)} %bitcast.109) | data formatting | bytes 12582912
  210.1 28.7 %all-gather.3.cloned.1.call-done = bf16[384,6144]{0,1:T(8,128)(2,1)} async-done(((bf16[384,192]{0,1:T(8,128)(2,1)}), bf16[384,6144]{0,1:T(8,128)(2,1)}) %all-gather.3.cloned.1.call-update) | async-done | bytes 4718608 | tf_op jit(solution)/shard_map/all_gather | solution.py:131
  238.8 6.3 %fusion.58 = f32[384,512]{1,0:T(8,128)S(1)} fusion(bf16[384,6144]{0,1:T(8,128)(2,1)} %all-gather.3.cloned.1.call-done, bf16[6144,512]{1,0:T(8,128)(2,1)} %bitcast.105), kind=kOutput, calls=%fused_computation.109 | convolution fusion | flops 2415919104 | bytes 11796480 | tf_op jit(solution)/shard_map/dot_general | solution.py:130
  252.7 34.1 %all-to-all-done.3 = bf16[32,2,24576]{2,1,0:T(2,128)(2,1)} async-done(((bf16[32,2,24576]{2,1,0:T(2,128)(2,1)}), bf16[32,2,24576]{2,1,0:T(2,128)(2,1)}, u32[]{:S(2)}, u32[]{:S(2)}) %all-to-all-start.3) | async-done | bytes 3145760 | tf_op jit(solution)/shard_map/all_to_all | solution.py:136
  287.7 6.6 %all-to-all-start.4 = ((f32[32,768,8]{1,2,0:T(8,128)}), f32[32,768,8]{1,2,0:T(8,128)S(1)}, u32[]{:S(2)}, u32[]{:S(2)}) async-start(f32[32,768,8]{1,2,0:T(8,128)} %broadcast_in_dim.180), calls=%async_computation.4 | async-start | bytes 1572864 | tf_op jit(solution)/shard_map/all_to_all | solution.py:17
  294.3 5.7 %broadcast_select_fusion = bf16[32,1,32768]{2,1,0:T(2,128)(2,1)} fusion(pred[32]{0:T(512)(128)(4,1)S(1)} %iota_compare_fusion.7, bf16[32768]{0:T(1024)(128)(2,1)S(1)} %fusion.28), kind=kLoop, calls=%fused_computation.2 | loop fusion | flops 1048576 | bytes 2162720 | tf_op jit(solution)/shard_map/jit(_where)/select_n | solution.py:162
  299.9 14.4 %reduce.11 = bf16[32,32768]{1,0:T(8,128)(2,1)} reduce(bf16[32,1,32768]{2,1,0:T(2,128)(2,1)} %broadcast_select_fusion, bf16[]{:T(256)} %broadcast.197), dimensions={1}, to_apply=%broadcast_select_fusion.reduce_sub_computation | reduce | bytes 4194306 | tf_op jit(solution)/shard_map/jit(_where)/select_n | solution.py:162
  314.4 4.5 reshape.335
  318.9 9.6 %all-to-all-start.6 = ((bf16[32,2,16384]{2,1,0:T(2,128)(2,1)}), bf16[32,2,16384]{2,1,0:T(2,128)(2,1)}, u32[]{:S(2)}, u32[]{:S(2)}) async-start(bf16[32,2,16384]{2,1,0:T(2,128)(2,1)} %reshape.335), calls=%async_computation.6 | async-start | bytes 4194304 | tf_op jit(solution)/shard_map/all_to_all | solution.py:165
  328.5 19.0 %reshape.334 = bf16[6144,1,256]{2,1,0:T(2,128)(2,1)} reshape(bf16[32,2,24576]{2,1,0:T(2,128)(2,1)} %all-to-all-done.3) | data formatting | bytes 6291456
  354.0 50.7 %all-gather.5.cloned.1.call-done = bf16[384,8192]{1,0:T(8,128)(2,1)} async-done(((bf16[384,256]{1,0:T(8,128)(2,1)}), bf16[384,8192]{1,0:T(8,128)(2,1)}) %all-gather.5.cloned.1.call-update) | async-done | bytes 6291472 | tf_op jit(solution)/shard_map/all_gather | solution.py:139
  404.7 5.9 %fusion.59 = f32[384,192]{0,1:T(8,128)S(1)} fusion(bf16[384,8192]{1,0:T(8,128)(2,1)} %all-gather.5.cloned.1.call-done, bf16[8192,192]{0,1:T(8,128)(2,1)} %bitcast.111), kind=kOutput, calls=%fused_computation.110 | convolution fusion | flops 1207959552 | bytes 9732096 | tf_op jit(solution)/shard_map/dot_general | solution.py:137
  413.7 6.4 %all-to-all-start.5 = ((bf16[8,192,768]{2,1,0:T(8,128)(2,1)}), bf16[8,192,768]{2,1,0:T(8,128)(2,1)}, u32[]{:S(2)}, u32[]{:S(2)}) async-start(bf16[8,192,768]{2,1,0:T(8,128)(2,1)} %broadcast_in_dim.187), calls=%async_computation.5 | async-start | bytes 4718592 | tf_op jit(solution)/shard_map/all_to_all | solution.py:17
  420.4 10.5 %reshape.336 = bf16[32,1,32768]{2,1,0:T(2,128)(2,1)} reshape(bf16[32,2,16384]{2,1,0:T(2,128)(2,1)} %all-to-all-done.6) | data formatting | bytes 4194304
  430.8 4.5 fusion.7
  436.0 13.2 %all-to-all-done.5 = bf16[8,192,768]{2,1,0:T(8,128)(2,1)} async-done(((bf16[8,192,768]{2,1,0:T(8,128)(2,1)}), bf16[8,192,768]{2,1,0:T(8,128)(2,1)}, u32[]{:S(2)}, u32[]{:S(2)}) %all-to-all-start.5) | async-done | bytes 2359328 | tf_op jit(solution)/shard_map/all_to_all | solution.py:17
  (107 shorter events, 47.0 us)
Async XLA Ops:
  7.2 50.8 %copy-start = (bf16[768,192]{0,1:T(8,128)(2,1)S(1)}, bf16[768,192]{0,1:T(8,128)(2,1)}, u32[]{:S(2)}) copy-start(bf16[768,192]{0,1:T(8,128)(2,1)} %param.23) | copy-start | bytes 884740
  61.1 7.3 %copy-start.3 = (s32[768,2]{0,1:T(2,128)S(1)}, s32[768,2]{0,1:T(2,128)}, u32[]{:S(2)}) copy-start(s32[768,2]{0,1:T(2,128)} %param.26) | copy-start | bytes 18436
  61.1 7.9 %copy-start.2 = (bf16[768,192]{0,1:T(8,128)(2,1)S(1)}, bf16[768,192]{0,1:T(8,128)(2,1)}, u32[]{:S(2)}) copy-start(bf16[768,192]{0,1:T(8,128)(2,1)} %param.16) | copy-start | bytes 884740
  61.1 61.7 %all-to-all-start.1 = ((f32[8,768,192]{1,2,0:T(8,128)}), f32[8,768,192]{1,2,0:T(8,128)}, u32[]{:S(2)}, u32[]{:S(2)}) async-start(f32[8,768,192]{1,2,0:T(8,128)} %broadcast_in_dim.174), calls=%async_computation.1 | async-start | bytes 9437184 | tf_op jit(solution)/shard_map/all_to_all | solution.py:17
  125.5 14.1 %copy-start.5 = (f32[192]{0:T(256)S(1)}, f32[192]{0:T(256)}, u32[]{:S(2)}) copy-start(f32[192]{0:T(256)} %param.24) | copy-start | bytes 2308
  126.7 12.9 %all-to-all-start.2 = ((f32[32,1,768]{2,1,0:T(1,128)}), f32[32,1,768]{2,1,0:T(1,128)S(1)}, u32[]{:S(2)}, u32[]{:S(2)}) async-start(f32[32,1,768]{2,1,0:T(1,128)} %broadcast_in_dim.176), calls=%async_computation.2 | async-start | bytes 196608 | tf_op jit(solution)/shard_map/all_to_all | solution.py:17
  130.6 108.2 %all-gather.3.cloned.1.call-start = ((), (), s32[]{:S(2)}) async-start(), calls=%async_computation.7 | async-start | bytes 4866048 | tf_op jit(solution)/shard_map/all_gather | solution.py:131
  198.5 88.2 %all-to-all-start.3 = ((bf16[32,2,24576]{2,1,0:T(2,128)(2,1)}), bf16[32,2,24576]{2,1,0:T(2,128)(2,1)}, u32[]{:S(2)}, u32[]{:S(2)}) async-start(bf16[32,2,24576]{2,1,0:T(2,128)(2,1)} %reshape.333), calls=%async_computation.3 | async-start | bytes 6291456 | tf_op jit(solution)/shard_map/all_to_all | solution.py:136
  203.3 201.4 %all-gather.5.cloned.1.call-start = ((), (), s32[]{:S(2)}) async-start(), calls=%async_computation.8 | async-start | bytes 6488064 | tf_op jit(solution)/shard_map/all_gather | solution.py:139
  238.8 7.1 %copy-start.7 = (s32[32]{0:T(128)S(1)}, s32[32]{0:T(128)}, u32[]{:S(2)}) copy-start(s32[32]{0:T(128)} %param.30) | copy-start | bytes 388
  238.8 9.0 %copy-start.8 = (s32[32]{0:T(128)S(1)}, s32[32]{0:T(128)}, u32[]{:S(2)}) copy-start(s32[32]{0:T(128)} %param.31) | copy-start | bytes 388
  238.8 9.7 %copy-start.6 = (s32[32]{0:T(128)S(1)}, s32[32]{0:T(128)}, u32[]{:S(2)}) copy-start(s32[32]{0:T(128)} %param.29) | copy-start | bytes 388
  238.8 13.2 %copy-start.4 = (bf16[192,8]{0,1:T(8,128)(2,1)S(1)}, bf16[192,8]{0,1:T(8,128)(2,1)}, u32[]{:S(2)}) copy-start(bf16[192,8]{0,1:T(8,128)(2,1)} %param.25) | copy-start | bytes 9220
  287.7 31.2 %all-to-all-start.4 = ((f32[32,768,8]{1,2,0:T(8,128)}), f32[32,768,8]{1,2,0:T(8,128)S(1)}, u32[]{:S(2)}, u32[]{:S(2)}) async-start(f32[32,768,8]{1,2,0:T(8,128)} %broadcast_in_dim.180), calls=%async_computation.4 | async-start | bytes 1572864 | tf_op jit(solution)/shard_map/all_to_all | solution.py:17
  318.9 93.1 %all-to-all-start.6 = ((bf16[32,2,16384]{2,1,0:T(2,128)(2,1)}), bf16[32,2,16384]{2,1,0:T(2,128)(2,1)}, u32[]{:S(2)}, u32[]{:S(2)}) async-start(bf16[32,2,16384]{2,1,0:T(2,128)(2,1)} %reshape.335), calls=%async_computation.6 | async-start | bytes 4194304 | tf_op jit(solution)/shard_map/all_to_all | solution.py:165
  413.7 35.5 %all-to-all-start.5 = ((bf16[8,192,768]{2,1,0:T(8,128)(2,1)}), bf16[8,192,768]{2,1,0:T(8,128)(2,1)}, u32[]{:S(2)}, u32[]{:S(2)}) async-start(bf16[8,192,768]{2,1,0:T(8,128)(2,1)} %broadcast_in_dim.187), calls=%async_computation.5 | async-start | bytes 4718592 | tf_op jit(solution)/shard_map/all_to_all | solution.py:17
  449.2 3.4 copy-start.1
Sparse Core Ops, SparseCore 0:
  143.0 95.7 all-gather.2
  246.0 158.6 all-gather.4
where the time goes:
time: 462 us; the launch traced here: 459 us
  waiting for transfers between devices  185 us (40%)
  local copies, waits for them, and re-layouts  85.5 us (19%)
  other arithmetic  67.1 us (15%)
  blocking collectives  43 us (9%)
  starting transfers between devices  38.8 us (8%)
  matrix products  22.7 us (5%)
  between operations  17 us (4%)
    all_to_all x4, waiting for transfers between devices, from_everyone(): return lax.all_to_all(copies, axis, split_axis=0, concat_axis=0, tiled=True)  71.9 us
    unnamed x33, local copies, waits for them, and re-layouts  71 us
    all_gather x1, waiting for transfers between devices, local(): lax.all_gather(act, 'rep', axis=1, tiled=True)  50.7 us
    all_to_all x1, blocking collectives, from_everyone(): return lax.all_to_all(copies, axis, split_axis=0, concat_axis=0, tiled=True)  43 us
    all_to_all x1, waiting for transfers between devices, local(): lax.all_to_all(w_down, 'rep', split_axis=2, concat_axis=1, tiled=True)[0]  34.1 us
    unnamed x2, other arithmetic  33.4 us
    all_gather x1, waiting for transfers between devices, local(): lax.all_gather(picked, 'rep', axis=1, tiled=True)  28.7 us
    all_to_all x4, starting transfers between devices, from_everyone(): return lax.all_to_all(copies, axis, split_axis=0, concat_axis=0, tiled=True)  24.1 us
  transfers between devices with their start and end apart: 8, of which 6 were waited for; matrix products, arithmetic and copies ran while one was open for 33% of the time, Pallas kernels for 0%

commit v1 on v0

--- a/solution.py
+++ b/solution.py
@@ -127,11 +127,13 @@
     ff_local = w_in.shape[3]
     w_flat = w_in[0].reshape(D, 2 * ff_local)
     picked = jnp.where(live[:, None], u_rows[token_of_slot], jnp.zeros((), jnp.bfloat16))
-    gate_up = jnp.dot(
-        lax.all_gather(picked, "rep", axis=1, tiled=True),
-        w_flat,
-        preferred_element_type=jnp.float32,
-    )
+
+    def zones_convert(chunk, dim_no=1):
+        finding = jnp.stack(jax.lax.psum(1, axis_name="rep") * [chunk])
+        z1 = jax.lax.all_to_all(finding, concat_axis=0, axis_name="rep", split_axis=0)
+        return jnp.concatenate(z1, dim_no)
+
+    gate_up = jnp.dot(zones_convert(picked), w_flat, preferred_element_type=jnp.float32)
     act = (jax.nn.silu(gate_up[:, :ff_local]) * gate_up[:, ff_local:]).astype(jnp.bfloat16)
     down_rows = lax.all_to_all(w_down, "rep", split_axis=2, concat_axis=1, tiled=True)[0]
     expert_out = lax.dot_general(

time: 462 us -> 504 us (1.091)
  waiting for transfers between devices: 185 us -> 220 us
  starting transfers between devices: 38.8 us -> 47.4 us
    all_to_all x0 -> x1, waiting for transfers between devices: none -> 51.7 us  [zones_convert(): jax.lax.all_to_all(finding, concat_axis=0, axis_name='rep', split_axis=0)]
    all_gather x1 -> x0, waiting for transfers between devices: 28.7 us -> none  [local(): lax.all_gather(picked, 'rep', axis=1, tiled=True)]
    all_to_all x1, waiting for transfers between devices: 34.1 us -> 60.4 us  [local(): lax.all_to_all(w_down, 'rep', split_axis=2, concat_axis=1, tiled=True)[0]]
    all_gather x1, waiting for transfers between devices: 50.7 us -> 33.9 us  [local(): lax.all_gather(act, 'rep', axis=1, tiled=True)]
    all_to_all x0 -> x1, starting transfers between devices: none -> 5.04 us  [zones_convert(): jax.lax.all_to_all(finding, concat_axis=0, axis_name='rep', split_axis=0)]
  transfers between devices with their start and end apart: 8 -> 8, of which waited for: 6 -> 7; matrix products, arithmetic and copies ran while one was open for 33% -> 30% of each run, Pallas kernels for 0% -> 0%
where the time goes in v1:
time: 504 us; the launch traced here: 501 us
  waiting for transfers between devices  220 us (44%)
  local copies, waits for them, and re-layouts  85 us (17%)
  other arithmetic  67 us (13%)
  starting transfers between devices  47.4 us (9%)
  blocking collectives  43 us (9%)
  matrix products  21.4 us (4%)
  between operations  17 us (3%)
    all_to_all x4, waiting for transfers between devices, from_everyone(): return lax.all_to_all(copies, axis, split_axis=0, concat_axis=0, tiled=True)  74 us
    unnamed x33, local copies, waits for them, and re-layouts  68.1 us
    all_to_all x1, waiting for transfers between devices, local(): lax.all_to_all(w_down, 'rep', split_axis=2, concat_axis=1, tiled=True)[0]  60.4 us
    all_to_all x1, waiting for transfers between devices, zones_convert(): jax.lax.all_to_all(finding, concat_axis=0, axis_name='rep', split_axis=0)  51.7 us
    all_to_all x1, blocking collectives, from_everyone(): return lax.all_to_all(copies, axis, split_axis=0, concat_axis=0, tiled=True)  43 us
    all_gather x1, waiting for transfers between devices, local(): lax.all_gather(act, 'rep', axis=1, tiled=True)  33.9 us
    unnamed x2, other arithmetic  33.3 us
    all_to_all x4, starting transfers between devices, from_everyone(): return lax.all_to_all(copies, axis, split_axis=0, concat_axis=0, tiled=True)  28.4 us
  transfers between devices with their start and end apart: 8, of which 7 were waited for; matrix products, arithmetic and copies ran while one was open for 30% of the time, Pallas kernels for 0%

profile of v1, /device:TPU:1, one launch (start us, length us, event | category | flops | bytes accessed | tf_op | source)
XLA Modules:
  0.0 501.0 jit_solution(16855401401481794313)
XLA Ops:
  15.0 43.0 %all_to_all.55 = bf16[32,24,768]{2,1,0:T(8,128)(2,1)S(1)} all-to-all(bf16[32,24,768]{2,1,0:T(8,128)(2,1)S(1)} %broadcast_in_dim.173), channel_id=1, replica_groups=mesh['rep'=32,'hx'=8] {'rep'}, dimensions={0} | all-to-all | bytes 2359296 | tf_op jit(solution)/shard_map/all_to_all | solution.py:17
  61.1 7.3 %all-to-all-start.1 = ((f32[8,768,192]{1,2,0:T(8,128)}), f32[8,768,192]{1,2,0:T(8,128)}, u32[]{:S(2)}, u32[]{:S(2)}) async-start(f32[8,768,192]{1,2,0:T(8,128)} %broadcast_in_dim.174), calls=%async_computation.1 | async-start | bytes 9437184 | tf_op jit(solution)/shard_map/all_to_all | solution.py:17
  72.7 50.1 %all-to-all-done.1 = f32[8,768,192]{1,2,0:T(8,128)} async-done(((f32[8,768,192]{1,2,0:T(8,128)}), f32[8,768,192]{1,2,0:T(8,128)}, u32[]{:S(2)}, u32[]{:S(2)}) %all-to-all-start.1) | async-done | bytes 4718624 | tf_op jit(solution)/shard_map/all_to_all | solution.py:17
  131.0 8.6 %all-to-all-done.2 = f32[32,1,768]{2,1,0:T(1,128)S(1)} async-done(((f32[32,1,768]{2,1,0:T(1,128)}), f32[32,1,768]{2,1,0:T(1,128)S(1)}, u32[]{:S(2)}, u32[]{:S(2)}) %all-to-all-start.2) | async-done | bytes 98336 | tf_op jit(solution)/shard_map/all_to_all | solution.py:17
  145.1 5.0 %all-to-all-start.3 = ((bf16[32,384,192]{1,2,0:T(8,128)(2,1)}), bf16[32,384,192]{1,2,0:T(8,128)(2,1)}, u32[]{:S(2)}, u32[]{:S(2)}) async-start(bf16[32,384,192]{1,2,0:T(8,128)(2,1)} %stack.2), calls=%async_computation.3 | async-start | bytes 9437184 | tf_op jit(solution)/shard_map/all_to_all | solution.py:133
  150.2 14.0 %copy.95 = bf16[1,256,6144]{1,0,2:T(2,128)(2,1)} copy(bf16[1,256,6144]{2,1,0:T(8,128)(2,1)} %param.28) | data formatting | bytes 6291456 | tf_op args[12]
  164.6 33.2 %reduce.10 = bf16[6144,256]{1,0:T(8,128)(2,1)} reduce(bf16[6144,1,256]{2,1,0:T(2,128)(2,1)} %bitcast.109, bf16[]{:T(256)} %broadcast.202), dimensions={1}, to_apply=%bitcast.91.reduce_sub_computation | reduce | bytes 6291458
  197.9 7.8 %reshape.349 = bf16[32,2,24576]{2,1,0:T(2,128)(2,1)} reshape(bf16[6144,256]{1,0:T(8,128)(2,1)} %reduce.10) | data formatting | bytes 6291456
  205.7 51.7 %all-to-all-done.3 = bf16[32,384,192]{1,2,0:T(8,128)(2,1)} async-done(((bf16[32,384,192]{1,2,0:T(8,128)(2,1)}), bf16[32,384,192]{1,2,0:T(8,128)(2,1)}, u32[]{:S(2)}, u32[]{:S(2)}) %all-to-all-start.3) | async-done | bytes 4718624 | tf_op jit(solution)/shard_map/all_to_all | solution.py:133
  257.4 5.9 %all-to-all-start.4 = ((bf16[32,2,24576]{2,1,0:T(2,128)(2,1)}), bf16[32,2,24576]{2,1,0:T(2,128)(2,1)}, u32[]{:S(2)}, u32[]{:S(2)}) async-start(bf16[32,2,24576]{2,1,0:T(2,128)(2,1)} %reshape.349), calls=%async_computation.4 | async-start | bytes 6291456 | tf_op jit(solution)/shard_map/all_to_all | solution.py:138
  267.2 5.0 fusion.58
  279.8 60.4 %all-to-all-done.4 = bf16[32,2,24576]{2,1,0:T(2,128)(2,1)} async-done(((bf16[32,2,24576]{2,1,0:T(2,128)(2,1)}), bf16[32,2,24576]{2,1,0:T(2,128)(2,1)}, u32[]{:S(2)}, u32[]{:S(2)}) %all-to-all-start.4) | async-done | bytes 3145760 | tf_op jit(solution)/shard_map/all_to_all | solution.py:138
  341.2 9.6 %all-to-all-start.5 = ((f32[32,768,8]{1,2,0:T(8,128)}), f32[32,768,8]{1,2,0:T(8,128)S(1)}, u32[]{:S(2)}, u32[]{:S(2)}) async-start(f32[32,768,8]{1,2,0:T(8,128)} %broadcast_in_dim.180), calls=%async_computation.5 | async-start | bytes 1572864 | tf_op jit(solution)/shard_map/all_to_all | solution.py:17
  350.8 5.7 %broadcast_select_fusion = bf16[32,1,32768]{2,1,0:T(2,128)(2,1)} fusion(pred[32]{0:T(512)(128)(4,1)S(1)} %iota_compare_fusion.7, bf16[32768]{0:T(1024)(128)(2,1)S(1)} %fusion.28), kind=kLoop, calls=%fused_computation.2 | loop fusion | flops 1048576 | bytes 2162720 | tf_op jit(solution)/shard_map/jit(_where)/select_n | solution.py:164
  356.5 14.4 %reduce.11 = bf16[32,32768]{1,0:T(8,128)(2,1)} reduce(bf16[32,1,32768]{2,1,0:T(2,128)(2,1)} %broadcast_select_fusion, bf16[]{:T(256)} %broadcast.202), dimensions={1}, to_apply=%broadcast_select_fusion.reduce_sub_computation | reduce | bytes 4194306 | tf_op jit(solution)/shard_map/jit(_where)/select_n | solution.py:164
  370.9 4.5 reshape.351
  377.5 8.0 %all-to-all-start.7 = ((bf16[32,2,16384]{2,1,0:T(2,128)(2,1)}), bf16[32,2,16384]{2,1,0:T(2,128)(2,1)}, u32[]{:S(2)}, u32[]{:S(2)}) async-start(bf16[32,2,16384]{2,1,0:T(2,128)(2,1)} %reshape.351), calls=%async_computation.7 | async-start | bytes 4194304 | tf_op jit(solution)/shard_map/all_to_all | solution.py:167
  385.5 19.0 %reshape.350 = bf16[6144,1,256]{2,1,0:T(2,128)(2,1)} reshape(bf16[32,2,24576]{2,1,0:T(2,128)(2,1)} %all-to-all-done.4) | data formatting | bytes 6291456
  411.0 33.9 %all-gather.2.cloned.1.call-done = bf16[384,8192]{1,0:T(8,128)(2,1)} async-done(((bf16[384,256]{1,0:T(8,128)(2,1)}), bf16[384,8192]{1,0:T(8,128)(2,1)}) %all-gather.2.cloned.1.call-update) | async-done | bytes 6291472 | tf_op jit(solution)/shard_map/all_gather | solution.py:141
  444.9 5.9 %fusion.59 = f32[384,192]{0,1:T(8,128)S(1)} fusion(bf16[384,8192]{1,0:T(8,128)(2,1)} %all-gather.2.cloned.1.call-done, bf16[8192,192]{0,1:T(8,128)(2,1)} %bitcast.114), kind=kOutput, calls=%fused_computation.110 | convolution fusion | flops 1207959552 | bytes 9732096 | tf_op jit(solution)/shard_map/dot_general | solution.py:139
  453.9 7.7 %all-to-all-start.6 = ((bf16[8,192,768]{2,1,0:T(8,128)(2,1)}), bf16[8,192,768]{2,1,0:T(8,128)(2,1)}, u32[]{:S(2)}, u32[]{:S(2)}) async-start(bf16[8,192,768]{2,1,0:T(8,128)(2,1)} %broadcast_in_dim.187), calls=%async_computation.6 | async-start | bytes 4718592 | tf_op jit(solution)/shard_map/all_to_all | solution.py:17
  461.9 10.5 %reshape.352 = bf16[32,1,32768]{2,1,0:T(2,128)(2,1)} reshape(bf16[32,2,16384]{2,1,0:T(2,128)(2,1)} %all-to-all-done.7) | data formatting | bytes 4194304
  472.3 4.5 fusion.7
  477.5 13.2 %all-to-all-done.6 = bf16[8,192,768]{2,1,0:T(8,128)(2,1)} async-done(((bf16[8,192,768]{2,1,0:T(8,128)(2,1)}), bf16[8,192,768]{2,1,0:T(8,128)(2,1)}, u32[]{:S(2)}, u32[]{:S(2)}) %all-to-all-start.6) | async-done | bytes 2359328 | tf_op jit(solution)/shard_map/all_to_all | solution.py:17
  (107 shorter events, 54.9 us)
Async XLA Ops:
  7.2 50.8 %copy-start = (bf16[768,192]{0,1:T(8,128)(2,1)S(1)}, bf16[768,192]{0,1:T(8,128)(2,1)}, u32[]{:S(2)}) copy-start(bf16[768,192]{0,1:T(8,128)(2,1)} %param.23) | copy-start | bytes 884740
  61.1 7.3 %copy-start.3 = (s32[768,2]{0,1:T(2,128)S(1)}, s32[768,2]{0,1:T(2,128)}, u32[]{:S(2)}) copy-start(s32[768,2]{0,1:T(2,128)} %param.26) | copy-start | bytes 18436
  61.1 7.9 %copy-start.2 = (bf16[768,192]{0,1:T(8,128)(2,1)S(1)}, bf16[768,192]{0,1:T(8,128)(2,1)}, u32[]{:S(2)}) copy-start(bf16[768,192]{0,1:T(8,128)(2,1)} %param.16) | copy-start | bytes 884740
  61.1 61.7 %all-to-all-start.1 = ((f32[8,768,192]{1,2,0:T(8,128)}), f32[8,768,192]{1,2,0:T(8,128)}, u32[]{:S(2)}, u32[]{:S(2)}) async-start(f32[8,768,192]{1,2,0:T(8,128)} %broadcast_in_dim.174), calls=%async_computation.1 | async-start | bytes 9437184 | tf_op jit(solution)/shard_map/all_to_all | solution.py:17
  125.5 14.1 %copy-start.5 = (f32[192]{0:T(256)S(1)}, f32[192]{0:T(256)}, u32[]{:S(2)}) copy-start(f32[192]{0:T(256)} %param.24) | copy-start | bytes 2308
  126.7 12.9 %all-to-all-start.2 = ((f32[32,1,768]{2,1,0:T(1,128)}), f32[32,1,768]{2,1,0:T(1,128)S(1)}, u32[]{:S(2)}, u32[]{:S(2)}) async-start(f32[32,1,768]{2,1,0:T(1,128)} %broadcast_in_dim.176), calls=%async_computation.2 | async-start | bytes 196608 | tf_op jit(solution)/shard_map/all_to_all | solution.py:17
  145.1 112.3 %all-to-all-start.3 = ((bf16[32,384,192]{1,2,0:T(8,128)(2,1)}), bf16[32,384,192]{1,2,0:T(8,128)(2,1)}, u32[]{:S(2)}, u32[]{:S(2)}) async-start(bf16[32,384,192]{1,2,0:T(8,128)(2,1)} %stack.2), calls=%async_computation.3 | async-start | bytes 9437184 | tf_op jit(solution)/shard_map/all_to_all | solution.py:133
  257.4 82.8 %all-to-all-start.4 = ((bf16[32,2,24576]{2,1,0:T(2,128)(2,1)}), bf16[32,2,24576]{2,1,0:T(2,128)(2,1)}, u32[]{:S(2)}, u32[]{:S(2)}) async-start(bf16[32,2,24576]{2,1,0:T(2,128)(2,1)} %reshape.349), calls=%async_computation.4 | async-start | bytes 6291456 | tf_op jit(solution)/shard_map/all_to_all | solution.py:138
  263.3 181.7 %all-gather.2.cloned.1.call-start = ((), (), s32[]{:S(2)}) async-start(), calls=%async_computation.8 | async-start | bytes 6488064 | tf_op jit(solution)/shard_map/all_gather | solution.py:141
  267.2 5.9 %copy-start.7 = (s32[32]{0:T(128)S(1)}, s32[32]{0:T(128)}, u32[]{:S(2)}) copy-start(s32[32]{0:T(128)} %param.30) | copy-start | bytes 388
  267.2 7.8 %copy-start.8 = (s32[32]{0:T(128)S(1)}, s32[32]{0:T(128)}, u32[]{:S(2)}) copy-start(s32[32]{0:T(128)} %param.31) | copy-start | bytes 388
  267.2 8.4 %copy-start.6 = (s32[32]{0:T(128)S(1)}, s32[32]{0:T(128)}, u32[]{:S(2)}) copy-start(s32[32]{0:T(128)} %param.29) | copy-start | bytes 388
  267.2 11.9 %copy-start.4 = (bf16[192,8]{0,1:T(8,128)(2,1)S(1)}, bf16[192,8]{0,1:T(8,128)(2,1)}, u32[]{:S(2)}) copy-start(bf16[192,8]{0,1:T(8,128)(2,1)} %param.25) | copy-start | bytes 9220
  341.2 36.3 %all-to-all-start.5 = ((f32[32,768,8]{1,2,0:T(8,128)}), f32[32,768,8]{1,2,0:T(8,128)S(1)}, u32[]{:S(2)}, u32[]{:S(2)}) async-start(f32[32,768,8]{1,2,0:T(8,128)} %broadcast_in_dim.180), calls=%async_computation.5 | async-start | bytes 1572864 | tf_op jit(solution)/shard_map/all_to_all | solution.py:17
  377.5 74.8 %all-to-all-start.7 = ((bf16[32,2,16384]{2,1,0:T(2,128)(2,1)}), bf16[32,2,16384]{2,1,0:T(2,128)(2,1)}, u32[]{:S(2)}, u32[]{:S(2)}) async-start(bf16[32,2,16384]{2,1,0:T(2,128)(2,1)} %reshape.351), calls=%async_computation.7 | async-start | bytes 4194304 | tf_op jit(solution)/shard_map/all_to_all | solution.py:167
  453.9 36.8 %all-to-all-start.6 = ((bf16[8,192,768]{2,1,0:T(8,128)(2,1)}), bf16[8,192,768]{2,1,0:T(8,128)(2,1)}, u32[]{:S(2)}, u32[]{:S(2)}) async-start(bf16[8,192,768]{2,1,0:T(8,128)(2,1)} %broadcast_in_dim.187), calls=%async_computation.6 | async-start | bytes 4718592 | tf_op jit(solution)/shard_map/all_to_all | solution.py:17
  490.8 3.4 copy-start.1
Sparse Core Ops, SparseCore 0:
  273.1 171.7 all-gather.1
